TPU v7x, 32 devices: a whole 2x2x4 slice. The times are simulated.
32 devices in a mesh: gx: 8 (over z, core), gy: 4 (over y, x).
Axes of the slice: x: 2, y: 2, z: 4, core: 2. Of those that a mesh axis runs over, the one named last changes fastest.
Arguments:
- tokens: bfloat16 [64, 32, 8, 768], P('gx', 'gy'), may hold values from -64 to 64
- target: bfloat16 [64, 32, 8, 768], P('gx', 'gy'), may hold values from -4 to 4
- norm_gain: float32 [768], replicated, may hold values from 0.1 to 1.9
- qkv_weight: bfloat16 [768, 1152], P('gy'), may hold values from -4 to 4
- proj_weight: bfloat16 [384, 768], P('gy'), may hold values from -1.5 to 1.5
Outputs:
- block_out: bfloat16 [64, 32, 8, 768], P('gx', 'gy')
- qkv_grad: float32 [768, 1152], P('gy')
All inputs are finite; a program needn't handle non-finite values.
Results may differ from a plain program's by a relative error of at most 0.0094.
Values may be sent and summed in bfloat16 or wider, within the bound.
A program may use at most 64 MiB of HBM per device.

v0:
```python
import math
import jax
import jax.numpy as jnp
from jax import lax
from jax.sharding import PartitionSpec as P

HEADS = 12
HD = 32
WIN = 8
norm_eps = 1e-05


def shifted(x, axis, by):
    devices = lax.axis_size(axis)
    return lax.ppermute(x, axis, [(i, (i + by) % devices) for i in range(devices)])


def displace(volume, half_width):
    volume = jnp.roll(volume, -half_width, axis=2)
    upper_rows = shifted(volume[:half_width], "gx", -1)
    volume = jnp.concatenate([volume[half_width:], upper_rows], 0)
    upper_cols = shifted(volume[:, :half_width], "gy", -1)
    return jnp.concatenate([volume[:, half_width:], upper_cols], 1)


def restore(volume, half_width):
    lower_rows = shifted(volume[-half_width:], "gx", 1)
    volume = jnp.concatenate([lower_rows, volume[:-half_width]], 0)
    lower_cols = shifted(volume[:, -half_width:], "gy", 1)
    volume = jnp.concatenate([lower_cols, volume[:, :-half_width]], 1)
    return jnp.roll(volume, half_width, axis=2)


def into_windows(volume, window):
    ext_x, ext_y, ext_z, channels = volume.shape
    blocks = volume.reshape(ext_x, ext_y, ext_z // window, window, channels)
    return blocks.transpose(2, 0, 1, 3, 4).reshape(
        ext_z // window, ext_x * ext_y * window, channels
    )


def from_windows(windows, ext_x, ext_y, window):
    window_count = windows.shape[0]
    channels = windows.shape[2]
    blocks = windows.reshape(window_count, ext_x, ext_y, window, channels).transpose(1, 2, 0, 3, 4)
    return blocks.reshape(ext_x, ext_y, window_count * window, channels)


def head_probs(queries, keys_in, score_scale):
    scores = (
        jnp.einsum("wqd,wkd->wqk", queries, keys_in, preferred_element_type=jnp.float32)
        * score_scale
    )
    row_max = jnp.max(scores, -1, keepdims=True)
    exponent = jnp.exp(scores - row_max)
    return exponent / jnp.sum(exponent, -1, keepdims=True)


def shards(tokens, target, norm_gain, qkv_weight, proj_weight):
    window = WIN
    half_width = WIN // 2
    head_count = HEADS
    head_dim = HD
    inner_dim = HEADS * HD
    score_scale = HD ** (-0.5)
    ext_x, ext_y, ext_z, channels = tokens.shape
    total_tokens = ext_x * ext_y * ext_z * lax.axis_size("gx") * lax.axis_size("gy")
    loss_scale = 2.0 / math.sqrt(total_tokens)
    widened = tokens.astype(jnp.float32)
    token_mean = jnp.mean(widened, -1, keepdims=True)
    centred = widened - token_mean
    variance = jnp.mean(centred * centred, -1, keepdims=True)
    normed = (centred * lax.rsqrt(variance + norm_eps) * norm_gain).astype(jnp.bfloat16)
    windows_in = into_windows(displace(normed, half_width), window)
    window_count = windows_in.shape[0]
    window_tokens = windows_in.shape[1]
    flat_in = windows_in.reshape(-1, channels)
    qkv_whole = lax.all_gather(qkv_weight, "gy", axis=0, tiled=True)
    qkv_act = jnp.dot(flat_in, qkv_whole, preferred_element_type=jnp.float32).astype(jnp.bfloat16)
    qkv_act = qkv_act.reshape(window_count, window_tokens, 3 * inner_dim)

    def forward_head(head_idx, attn_buffer):
        queries = lax.dynamic_slice_in_dim(qkv_act, head_idx * head_dim, head_dim, 2)
        keys_in = lax.dynamic_slice_in_dim(qkv_act, inner_dim + head_idx * head_dim, head_dim, 2)
        values = lax.dynamic_slice_in_dim(qkv_act, 2 * inner_dim + head_idx * head_dim, head_dim, 2)
        attn_prob = head_probs(queries, keys_in, score_scale).astype(jnp.bfloat16)
        mixed = jnp.einsum(
            "wqk,wkd->wqd", attn_prob, values, preferred_element_type=jnp.float32
        ).astype(jnp.bfloat16)
        return lax.dynamic_update_slice_in_dim(attn_buffer, mixed, head_idx * head_dim, 2)

    attn_out = lax.fori_loop(
        0,
        head_count,
        forward_head,
        jnp.zeros((window_count, window_tokens, inner_dim), jnp.bfloat16),
    )
    proj_whole = lax.all_gather(proj_weight, "gy", axis=0, tiled=True)
    contract_cols = (((1,), (1,)), ((), ()))
    block_shift = jnp.dot(
        attn_out.reshape(-1, inner_dim), proj_whole, preferred_element_type=jnp.float32
    ).astype(jnp.bfloat16)
    block_shift = block_shift.reshape(window_count, window_tokens, channels)
    block_out = restore(from_windows(block_shift, ext_x, ext_y, window), half_width)
    grad_out = ((block_out.astype(jnp.float32) - target.astype(jnp.float32)) * loss_scale).astype(
        jnp.bfloat16
    )
    grad_shift = into_windows(displace(grad_out, half_width), window)
    grad_windows = lax.dot_general(
        grad_shift.reshape(-1, channels),
        proj_whole,
        contract_cols,
        preferred_element_type=jnp.float32,
    ).astype(jnp.bfloat16)
    grad_windows = grad_windows.reshape(window_count, window_tokens, inner_dim)

    def backward_head(head_idx, grad_buffer):
        queries = lax.dynamic_slice_in_dim(qkv_act, head_idx * head_dim, head_dim, 2)
        keys_in = lax.dynamic_slice_in_dim(qkv_act, inner_dim + head_idx * head_dim, head_dim, 2)
        values = lax.dynamic_slice_in_dim(qkv_act, 2 * inner_dim + head_idx * head_dim, head_dim, 2)
        attn_prob = head_probs(queries, keys_in, score_scale)
        prob_half = attn_prob.astype(jnp.bfloat16)
        grad_mixed = lax.dynamic_slice_in_dim(grad_windows, head_idx * head_dim, head_dim, 2)
        grad_probs = jnp.einsum(
            "wqd,wkd->wqk", grad_mixed, values, preferred_element_type=jnp.float32
        )
        grad_values = jnp.einsum(
            "wqk,wqd->wkd", prob_half, grad_mixed, preferred_element_type=jnp.float32
        ).astype(jnp.bfloat16)
        row_dot = jnp.sum(grad_probs * attn_prob, -1, keepdims=True)
        grad_scores = (attn_prob * (grad_probs - row_dot)).astype(jnp.bfloat16)
        grad_queries = (
            jnp.einsum("wqk,wkd->wqd", grad_scores, keys_in, preferred_element_type=jnp.float32)
            * score_scale
        ).astype(jnp.bfloat16)
        grad_keys = (
            jnp.einsum("wqk,wqd->wkd", grad_scores, queries, preferred_element_type=jnp.float32)
            * score_scale
        ).astype(jnp.bfloat16)
        grad_buffer = lax.dynamic_update_slice_in_dim(
            grad_buffer, grad_queries, head_idx * head_dim, 2
        )
        grad_buffer = lax.dynamic_update_slice_in_dim(
            grad_buffer, grad_keys, inner_dim + head_idx * head_dim, 2
        )
        return lax.dynamic_update_slice_in_dim(
            grad_buffer, grad_values, 2 * inner_dim + head_idx * head_dim, 2
        )

    grad_qkv = lax.fori_loop(
        0,
        head_count,
        backward_head,
        jnp.zeros((window_count, window_tokens, 3 * inner_dim), jnp.bfloat16),
    )
    grad_flat = grad_qkv.reshape(-1, 3 * inner_dim)
    contract_rows = (((0,), (0,)), ((), ()))
    shard_rows = qkv_weight.shape[0]
    local_grad = lax.dot_general(
        flat_in, grad_flat, contract_rows, preferred_element_type=jnp.float32
    )
    whole_grad = lax.psum(local_grad, ("gx", "gy"))
    qkv_grad = lax.dynamic_slice_in_dim(
        whole_grad, lax.axis_index("gy") * shard_rows, shard_rows, 0
    )
    return (block_out, qkv_grad)


def solution(mesh):
    in_specs = (
        P("gx", "gy", None, None),
        P("gx", "gy", None, None),
        P(),
        P("gy", None),
        P("gy", None),
    )
    out_specs = (P("gx", "gy", None, None), P("gy", None))
    return jax.shard_map(shards, mesh=mesh, in_specs=in_specs, out_specs=out_specs, check_vma=False)
```

profile of v0, /device:TPU:0, one launch (start us, length us, event | category | flops | bytes accessed | tf_op | source)
XLA Modules:
  0.0 313.7 jit_solution(8115496946814767307)
XLA Ops:
  8.0 1.3 convert_reduce_fusion
  10.7 4.6 %collective-permute-start = (bf16[4,8,8,768]{3,2,1,0:T(8,128)(2,1)S(1)}, bf16[4,8,8,768]{3,2,1,0:T(8,128)(2,1)S(1)}, u32[]{:S(2)}, u32[]{:S(2)}) collective-permute-start(bf16[4,8,8,768]{3,2,1,0:T(8,128)(2,1)S(1)} %get-tuple-element.239), channel_id=1, source_target_pairs={{0,28},{4,0},{8,4},{12,8},{16,12},{20,16},{24,20},{28,24},{1,29},{... | collective-permute-start | bytes 1179656 | tf_op jit(solution)/shard_map/ppermute | solution.py:15
  15.3 5.3 %collective-permute-done = bf16[4,8,8,768]{3,2,1,0:T(8,128)(2,1)S(1)} collective-permute-done((bf16[4,8,8,768]{3,2,1,0:T(8,128)(2,1)S(1)}, bf16[4,8,8,768]{3,2,1,0:T(8,128)(2,1)S(1)}, u32[]{:S(2)}, u32[]{:S(2)}) %collective-permute-start) | collective-permute-done | bytes 393248 | tf_op jit(solution)/shard_map/ppermute | solution.py:15
  20.7 2.5 collective-permute-start.1
  23.2 18.8 %all_gather.7 = bf16[384,768]{1,0:T(8,128)(2,1)} all-gather(bf16[96,768]{1,0:T(8,128)(2,1)S(1)} %copy-done.3), channel_id=1, replica_groups=mesh['gx'=8,'gy'=4] {'gy'}, dimensions={0}, use_global_device_ids=true | all-gather | bytes 737280 | tf_op jit(solution)/shard_map/all_gather | solution.py:98
  42.0 13.0 %all-gather.2.cloned.1.call-done = bf16[768,1152]{1,0:T(8,128)(2,1)} async-done(((bf16[192,1152]{1,0:T(8,128)(2,1)}), bf16[768,1152]{1,0:T(8,128)(2,1)}) %all-gather.2.cloned.1.call-update) | async-done | bytes 1769488 | tf_op jit(solution)/shard_map/all_gather | solution.py:78
  55.0 2.7 fusion.43
  57.7 11.2 %while.30 = (s32[]{:T(128)}, bf16[1,512,384]{1,2,0:T(8,128)(2,1)S(1)}, bf16[1,512,1152]{2,1,0:T(8,128)(2,1)S(1)}, s32[]{:T(128)}, s32[]{:T(128)}, /*index=5*/s32...) while((s32[]{:T(128)}, bf16[1,512,384]{1,2,0:T(8,128)(2,1)S(1)}, ...), condition=%wide.region_5.6_spmd, body=%wide.region_2.5_spmd.sunk | while | flops 35404812 | bytes 3582236 | solution.py:92
  68.9 1.7 convolution_convert_fusion.3
  70.7 9.0 %collective-permute-done.2 = bf16[4,8,8,768]{3,2,1,0:T(8,128)(2,1)S(1)} collective-permute-done((bf16[4,8,8,768]{3,2,1,0:T(8,128)(2,1)S(1)}, bf16[4,8,8,768]{3,2,1,0:T(8,128)(2,1)S(1)}, u32[]{:S(2)}, u32[]{:S(2)}) %collective-permute-start.2) | collective-permute-done | bytes 393248 | tf_op jit(solution)/shard_map/ppermute | solution.py:15
  79.7 1.5 collective-permute-start.3
  81.3 7.8 %collective-permute-done.3 = bf16[8,4,8,768]{3,2,1,0:T(8,128)(2,1)S(1)} collective-permute-done((bf16[8,4,8,768]{3,2,1,0:T(8,128)(2,1)S(1)}, bf16[8,4,8,768]{3,2,1,0:T(8,128)(2,1)S(1)}, u32[]{:S(2)}, u32[]{:S(2)}) %collective-permute-start.3) | collective-permute-done | bytes 393248 | tf_op jit(solution)/shard_map/ppermute | solution.py:15
  90.3 1.5 multiply_convert_fusion.1
  92.5 5.3 %collective-permute-done.4 = bf16[4,8,8,768]{3,2,1,0:T(8,128)(2,1)S(1)} collective-permute-done((bf16[4,8,8,768]{3,2,1,0:T(8,128)(2,1)S(1)}, bf16[4,8,8,768]{3,2,1,0:T(8,128)(2,1)S(1)}, u32[]{:S(2)}, u32[]{:S(2)}) %collective-permute-start.4) | collective-permute-done | bytes 393248 | tf_op jit(solution)/shard_map/ppermute | solution.py:15
  98.5 10.7 %collective-permute-done.5 = bf16[8,4,8,768]{3,2,1,0:T(8,128)(2,1)} collective-permute-done((bf16[8,4,8,768]{3,2,1,0:T(8,128)(2,1)S(1)}, bf16[8,4,8,768]{3,2,1,0:T(8,128)(2,1)}, u32[]{:S(2)}, u32[]{:S(2)}) %collective-permute-start.5) | collective-permute-done | bytes 393248 | tf_op jit(solution)/shard_map/ppermute | solution.py:15
  109.2 1.1 pad_maximum_fusion.3
  110.9 1.1 broadcast_in_dim.25
  112.0 49.0 %while.31 = (s32[]{:T(128)}, bf16[1,512,1152]{1,2,0:T(8,128)(2,1)}, bf16[1,512,1152]{2,1,0:T(8,128)(2,1)S(1)}, bf16[1,512,384]{2,1,0:T(8,128)(2,1)S(1)}, s32[]{:...) while((s32[]{:T(128)}, bf16[1,512,1152]{1,2,0:T(8,128)(2,1)}, ...), condition=%wide.region_10.11_spmd, body=%wide.region_6.10_spmd.sunk | while | flops 88160776 | bytes 9951548 | solution.py:150
  114.2 0.9 fusion.101
  115.2 0.9 fusion.102
  118.3 0.9 fusion.101
  119.3 0.9 fusion.102
  122.4 0.9 fusion.101
  123.3 0.9 fusion.102
  126.5 0.9 fusion.101
  127.4 0.9 fusion.102
  130.5 0.9 fusion.101
  131.5 0.9 fusion.102
  133.7 0.9 fusion.100
  134.6 1.0 fusion.101
  135.6 0.9 fusion.102
  138.7 0.9 fusion.101
  139.7 0.9 fusion.102
  141.9 0.9 fusion.100
  142.8 0.9 fusion.101
  143.8 0.9 fusion.102
  146.9 0.9 fusion.101
  147.8 0.9 fusion.102
  151.0 0.9 fusion.101
  151.9 0.9 fusion.102
  155.0 0.9 fusion.101
  156.0 0.9 fusion.102
  158.2 0.9 fusion.100
  159.1 0.9 fusion.101
  160.1 0.9 fusion.102
  161.0 4.2 %fusion.50 = f32[768,1152]{1,0:T(8,128)} fusion(bf16[512,768]{1,0:T(8,128)(2,1)S(1)} %bitcast.110, bf16[1,512,1152]{1,2,0:T(8,128)(2,1)} %get-tuple-element.203), kind=kOutput, calls=%fused_computation.66 | convolution fusion | flops 905969664 | bytes 5505024 | tf_op jit(solution)/shard_map/dot_general | solution.py:159
  165.3 139.4 %all-reduce.2.cloned.1.call-done = f32[768,1152]{1,0:T(8,128)} async-done(((f32[768,1152]{1,0:T(8,128)}), f32[768,1152]{1,0:T(8,128)}) %all-reduce.2.cloned.1.call-update) | async-done | bytes 3538960 | tf_op jit(solution)/shard_map/psum | solution.py:162
  304.7 2.1 constant_dynamic-slice_fusion
  (128 shorter events, 40.3 us)
Async XLA Ops:
  7.2 2.1 copy-start
  7.2 2.5 copy-start.4
  7.2 47.9 %all-gather.2.cloned.1.call-start = ((), (), s32[]{:S(2)}) async-start(), calls=%async_computation | async-start | bytes 2211840 | tf_op jit(solution)/shard_map/all_gather | solution.py:78
  7.9 296.8 %all-reduce.2.cloned.1.call-start = ((), (), s32[]{:S(2)}) async-start(), calls=%async_computation.1 | async-start | bytes 7077888 | tf_op jit(solution)/shard_map/psum | solution.py:162
  10.7 12.5 %copy-start.3 = (bf16[96,768]{1,0:T(8,128)(2,1)S(1)}, bf16[96,768]{1,0:T(8,128)(2,1)}, u32[]{:S(2)}) copy-start(bf16[96,768]{1,0:T(8,128)(2,1)} %param.13) | copy-start | bytes 442372
  10.7 9.9 %collective-permute-start = (bf16[4,8,8,768]{3,2,1,0:T(8,128)(2,1)S(1)}, bf16[4,8,8,768]{3,2,1,0:T(8,128)(2,1)S(1)}, u32[]{:S(2)}, u32[]{:S(2)}) collective-permute-start(bf16[4,8,8,768]{3,2,1,0:T(8,128)(2,1)S(1)} %get-tuple-element.239), channel_id=1, source_target_pairs={{0,28},{4,0},{8,4},{12,8},{16,12},{20,16},{24,20},{28,24},{1,29},{... | collective-permute-start | bytes 1179656 | tf_op jit(solution)/shard_map/ppermute | solution.py:15
  20.7 21.3 %collective-permute-start.1 = (bf16[8,4,8,768]{3,2,1,0:T(8,128)(2,1)S(1)}, bf16[8,4,8,768]{3,2,1,0:T(8,128)(2,1)S(1)}, u32[]{:S(2)}, u32[]{:S(2)}) collective-permute-start(bf16[8,4,8,768]{3,2,1,0:T(8,128)(2,1)S(1)} %get-tuple-element.237), channel_id=1, source_target_pairs={{0,3},{1,0},{2,1},{3,2},{4,7},{5,4},{6,5},{7,6},{8,11},{9,8},{10,9... | collective-permute-start | bytes 1179656 | tf_op jit(solution)/shard_map/ppermute | solution.py:15
  70.7 9.1 %collective-permute-start.2 = (bf16[4,8,8,768]{3,2,1,0:T(8,128)(2,1)S(1)}, bf16[4,8,8,768]{3,2,1,0:T(8,128)(2,1)S(1)}, u32[]{:S(2)}, u32[]{:S(2)}) collective-permute-start(bf16[4,8,8,768]{3,2,1,0:T(8,128)(2,1)S(1)} %bitcast.114), channel_id=1, source_target_pairs={{0,4},{4,8},{8,12},{12,16},{16,20},{20,24},{24,28},{28,0},{1,5},{5... | collective-permute-start | bytes 1179656 | tf_op jit(solution)/shard_map/ppermute | solution.py:15
  79.7 9.3 %collective-permute-start.3 = (bf16[8,4,8,768]{3,2,1,0:T(8,128)(2,1)S(1)}, bf16[8,4,8,768]{3,2,1,0:T(8,128)(2,1)S(1)}, u32[]{:S(2)}, u32[]{:S(2)}) collective-permute-start(bf16[8,4,8,768]{3,2,1,0:T(8,128)(2,1)S(1)} %fusion.55), channel_id=1, source_target_pairs={{0,1},{1,2},{2,3},{3,0},{4,5},{5,6},{6,7},{7,4},{8,9},{9,10},{10,1... | collective-permute-start | bytes 1179656 | tf_op jit(solution)/shard_map/ppermute | solution.py:15
  89.1 1.1 copy-start.2
  92.5 5.4 %collective-permute-start.4 = (bf16[4,8,8,768]{3,2,1,0:T(8,128)(2,1)S(1)}, bf16[4,8,8,768]{3,2,1,0:T(8,128)(2,1)S(1)}, u32[]{:S(2)}, u32[]{:S(2)}) collective-permute-start(bf16[4,8,8,768]{3,2,1,0:T(8,128)(2,1)S(1)} %get-tuple-element.229), channel_id=1, source_target_pairs={{0,28},{4,0},{8,4},{12,8},{16,12},{20,16},{24,20},{28,24},{1,29},{... | collective-permute-start | bytes 1179656 | tf_op jit(solution)/shard_map/ppermute | solution.py:15
  97.9 12.4 %copy-start.1 = (bf16[384,768]{1,0:T(8,128)(2,1)S(1)}, bf16[384,768]{1,0:T(8,128)(2,1)}, u32[]{:S(2)}) copy-start(bf16[384,768]{1,0:T(8,128)(2,1)} %all_gather.7) | copy-start | bytes 1769476
  97.9 11.4 %collective-permute-start.5 = (bf16[8,4,8,768]{3,2,1,0:T(8,128)(2,1)S(1)}, bf16[8,4,8,768]{3,2,1,0:T(8,128)(2,1)}, u32[]{:S(2)}, u32[]{:S(2)}) collective-permute-start(bf16[8,4,8,768]{3,2,1,0:T(8,128)(2,1)S(1)} %get-tuple-element.227), channel_id=1, source_target_pairs={{0,3},{1,0},{2,1},{3,2},{4,7},{5,4},{6,5},{7,6},{8,11},{9,8},{10,9... | collective-permute-start | bytes 1179656 | tf_op jit(solution)/shard_map/ppermute | solution.py:15
Sparse Core Ops, SparseCore 0:
  9.8 45.1 all-gather.1
  165.4 139.2 all-reduce.1
where the time goes:
time: 314 us
  waiting for transfers between devices  191 us (61%)
  matrix products  60.9 us (19%)
  blocking collectives  18.8 us (6%)
  between operations  14.3 us (5%)
  other arithmetic  13.7 us (4%)
  starting transfers between devices  9.39 us (3%)
  local copies, waits for them, and re-layouts  5.15 us (2%)
    psum x1, waiting for transfers between devices, shards(): whole_grad = lax.psum(local_grad, ('gx', 'gy'))  139 us
    ppermute x6, waiting for transfers between devices, shifted(): lax.ppermute(x, axis, [(i, (i + by) % devices) for i in range(devices)])  38.1 us
    all_gather x1, blocking collectives, shards(): proj_whole = lax.all_gather(proj_weight, 'gy', axis=0, tiled=True)  18.8 us
    all_gather x1, waiting for transfers between devices, shards(): qkv_whole = lax.all_gather(qkv_weight, 'gy', axis=0, tiled=True)  13 us
    dot_general x12, matrix products, backward_head(): jnp.einsum('wqk,wqd->wkd', grad_scores, queries, preferred_element_type=j...  11.3 us
    dot_general x12, matrix products, backward_head(): jnp.einsum('wqk,wqd->wkd', prob_half, grad_mixed, preferred_element_type=...  11.2 us
    dot_general x12, matrix products, backward_head(): jnp.einsum('wqk,wkd->wqd', grad_scores, keys_in, preferred_element_type=j...  11 us
    dot_general x24, matrix products, head_probs(): jnp.einsum('wqd,wkd->wqk', queries, keys_in, preferred_element_type=jnp.f...  9.39 us
  transfers between devices with their start and end apart: 8, of which 7 were waited for; matrix products, arithmetic and copies ran while one was open for 1% of the time, Pallas kernels for 0%

commit v1 on v0

--- a/solution.py
+++ b/solution.py
@@ -95,7 +95,12 @@
         forward_head,
         jnp.zeros((window_count, window_tokens, inner_dim), jnp.bfloat16),
     )
-    proj_whole = lax.all_gather(proj_weight, "gy", axis=0, tiled=True)
+    ring = [proj_weight]
+    for hop in range(3):
+        ring.append(lax.ppermute(ring[-1], "gy", [(dev, (dev + 1) % 4) for dev in range(4)]))
+    proj_whole = jnp.roll(
+        jnp.concatenate(ring[::-1], axis=0), (lax.axis_index("gy") + 1) * ring[0].shape[0], axis=0
+    )
     contract_cols = (((1,), (1,)), ((), ()))
     block_shift = jnp.dot(
         attn_out.reshape(-1, inner_dim), proj_whole, preferred_element_type=jnp.float32

time: 314 us -> 287 us (0.914)
  matrix products: 60.9 us -> 37.2 us
  blocking collectives: 18.8 us -> 0 us
  waiting for transfers between devices: 191 us -> 204 us
    all_gather x1 -> x0, blocking collectives: 18.8 us -> none  [shards(): proj_whole = lax.all_gather(proj_weight, 'gy', axis=0, tiled=True)]
    ppermute x0 -> x3, waiting for transfers between devices: none -> 16.4 us  [shards(): lax.ppermute(ring[-1], 'gy', [(dev, (dev + 1) % 4) for dev in range(4)])]
    all_gather x1, waiting for transfers between devices: 13 us -> 2.68 us  [shards(): qkv_whole = lax.all_gather(qkv_weight, 'gy', axis=0, tiled=True)]
    dot_general x12, matrix products: 11 us -> 3.62 us  [backward_head(): jnp.einsum('wqk,wkd->wqd', grad_scores, keys_in, preferred_element_type=j...]
    dot_general x12, matrix products: 11.3 us -> 3.94 us  [backward_head(): jnp.einsum('wqk,wqd->wkd', grad_scores, queries, preferred_element_type=j...]
    dot_general x12, matrix products: 11.2 us -> 4.18 us  [backward_head(): jnp.einsum('wqk,wqd->wkd', prob_half, grad_mixed, preferred_element_type=...]
    ppermute x6, waiting for transfers between devices: 38.1 us -> 44.3 us  [shifted(): lax.ppermute(x, axis, [(i, (i + by) % devices) for i in range(devices)])]
  transfers between devices with their start and end apart: 8 -> 11, of which waited for: 7 -> 10; matrix products, arithmetic and copies ran while one was open for 1% -> 1% of each run, Pallas kernels for 0% -> 0%
where the time goes in v1:
time: 287 us; the launch traced here: 286 us
  waiting for transfers between devices  204 us (71%)
  matrix products  37.2 us (13%)
  other arithmetic  14.4 us (5%)
  between operations  14.3 us (5%)
  starting transfers between devices  12.1 us (4%)
  local copies, waits for them, and re-layouts  4.21 us (1%)
    psum x1, waiting for transfers between devices, shards(): whole_grad = lax.psum(local_grad, ('gx', 'gy'))  140 us
    ppermute x6, waiting for transfers between devices, shifted(): lax.ppermute(x, axis, [(i, (i + by) % devices) for i in range(devices)])  44.3 us
    ppermute x3, waiting for transfers between devices, shards(): lax.ppermute(ring[-1], 'gy', [(dev, (dev + 1) % 4) for dev in range(4)])  16.4 us
    dot_general x24, matrix products, head_probs(): jnp.einsum('wqd,wkd->wqk', queries, keys_in, preferred_element_type=jnp.f...  9.63 us
    ppermute x6, starting transfers between devices, shifted(): lax.ppermute(x, axis, [(i, (i + by) % devices) for i in range(devices)])  9.22 us
  transfers between devices with their start and end apart: 11, of which 10 were waited for; matrix products, arithmetic and copies ran while one was open for 1% of the time, Pallas kernels for 0%

profile of v1, /device:TPU:0, one launch (start us, length us, event | category | flops | bytes accessed | tf_op | source)
XLA Modules:
  0.0 286.4 jit_solution(820773202929017001)
XLA Ops:
  7.2 0.7 all-gather.2.cloned.1.call-update
  8.0 1.3 convert_reduce_fusion
  10.7 4.6 %collective-permute-start = (bf16[4,8,8,768]{3,2,1,0:T(8,128)(2,1)S(1)}, bf16[4,8,8,768]{3,2,1,0:T(8,128)(2,1)S(1)}, u32[]{:S(2)}, u32[]{:S(2)}) collective-permute-start(bf16[4,8,8,768]{3,2,1,0:T(8,128)(2,1)S(1)} %get-tuple-element.239), channel_id=1, source_target_pairs={{0,28},{4,0},{8,4},{12,8},{16,12},{20,16},{24,20},{28,24},{1,29},{... | collective-permute-start | bytes 1179656 | tf_op jit(solution)/shard_map/ppermute | solution.py:15
  15.3 1.5 collective-permute-start.2
  16.8 4.9 %collective-permute-done.2 = bf16[96,768]{1,0:T(8,128)(2,1)S(1)} collective-permute-done((bf16[96,768]{1,0:T(8,128)(2,1)S(1)}, bf16[96,768]{1,0:T(8,128)(2,1)S(1)}, u32[]{:S(2)}, u32[]{:S(2)}) %collective-permute-start.2) | collective-permute-done | bytes 147488 | tf_op jit(solution)/shard_map/ppermute | solution.py:100
  21.7 1.3 collective-permute-start.3
  23.0 8.5 %collective-permute-done.3 = bf16[96,768]{1,0:T(8,128)(2,1)S(1)} collective-permute-done((bf16[96,768]{1,0:T(8,128)(2,1)S(1)}, bf16[96,768]{1,0:T(8,128)(2,1)S(1)}, u32[]{:S(2)}, u32[]{:S(2)}) %collective-permute-start.3) | collective-permute-done | bytes 147488 | tf_op jit(solution)/shard_map/ppermute | solution.py:100
  31.6 3.0 %collective-permute-start.1 = (bf16[8,4,8,768]{3,2,1,0:T(8,128)(2,1)S(1)}, bf16[8,4,8,768]{3,2,1,0:T(8,128)(2,1)S(1)}, u32[]{:S(2)}, u32[]{:S(2)}) collective-permute-start(bf16[8,4,8,768]{3,2,1,0:T(8,128)(2,1)S(1)} %get-tuple-element.237), channel_id=1, source_target_pairs={{0,3},{1,0},{2,1},{3,2},{4,7},{5,4},{6,5},{7,6},{8,11},{9,8},{10,9... | collective-permute-start | bytes 1179656 | tf_op jit(solution)/shard_map/ppermute | solution.py:15
  34.6 3.0 %collective-permute-done.4 = bf16[96,768]{1,0:T(8,128)(2,1)S(1)} collective-permute-done((bf16[96,768]{1,0:T(8,128)(2,1)S(1)}, bf16[96,768]{1,0:T(8,128)(2,1)S(1)}, u32[]{:S(2)}, u32[]{:S(2)}) %collective-permute-start.4) | collective-permute-done | bytes 147488 | tf_op jit(solution)/shard_map/ppermute | solution.py:100
  37.7 10.2 %collective-permute-done.1 = bf16[8,4,8,768]{3,2,1,0:T(8,128)(2,1)S(1)} collective-permute-done((bf16[8,4,8,768]{3,2,1,0:T(8,128)(2,1)S(1)}, bf16[8,4,8,768]{3,2,1,0:T(8,128)(2,1)S(1)}, u32[]{:S(2)}, u32[]{:S(2)}) %collective-permute-start.1) | collective-permute-done | bytes 393248 | tf_op jit(solution)/shard_map/ppermute | solution.py:15
  48.0 2.7 all-gather.2.cloned.1.call-done
  50.7 2.7 fusion.43
  53.4 11.1 %while.30 = (s32[]{:T(128)}, bf16[1,512,384]{1,2,0:T(8,128)(2,1)S(1)}, bf16[1,512,1152]{2,1,0:T(8,128)(2,1)S(1)}, s32[]{:T(128)}, s32[]{:T(128)}, /*index=5*/s32...) while((s32[]{:T(128)}, bf16[1,512,384]{1,2,0:T(8,128)(2,1)S(1)}, ...), condition=%wide.region_5.6_spmd, body=%wide.region_2.5_spmd.sunk | while | flops 35404812 | bytes 3582228 | solution.py:92
  64.6 0.6 convolution_convert_fusion.3
  65.3 9.9 %collective-permute-done.5 = bf16[4,8,8,768]{3,2,1,0:T(8,128)(2,1)S(1)} collective-permute-done((bf16[4,8,8,768]{3,2,1,0:T(8,128)(2,1)S(1)}, bf16[4,8,8,768]{3,2,1,0:T(8,128)(2,1)S(1)}, u32[]{:S(2)}, u32[]{:S(2)}) %collective-permute-start.5) | collective-permute-done | bytes 393248 | tf_op jit(solution)/shard_map/ppermute | solution.py:15
  75.3 1.3 collective-permute-start.6
  76.5 8.0 %collective-permute-done.6 = bf16[8,4,8,768]{3,2,1,0:T(8,128)(2,1)S(1)} collective-permute-done((bf16[8,4,8,768]{3,2,1,0:T(8,128)(2,1)S(1)}, bf16[8,4,8,768]{3,2,1,0:T(8,128)(2,1)S(1)}, u32[]{:S(2)}, u32[]{:S(2)}) %collective-permute-start.6) | collective-permute-done | bytes 393248 | tf_op jit(solution)/shard_map/ppermute | solution.py:15
  85.0 0.8 copy-done.1
  85.8 1.5 multiply_convert_fusion.1
  88.0 5.3 %collective-permute-done.7 = bf16[4,8,8,768]{3,2,1,0:T(8,128)(2,1)S(1)} collective-permute-done((bf16[4,8,8,768]{3,2,1,0:T(8,128)(2,1)S(1)}, bf16[4,8,8,768]{3,2,1,0:T(8,128)(2,1)S(1)}, u32[]{:S(2)}, u32[]{:S(2)}) %collective-permute-start.7) | collective-permute-done | bytes 393248 | tf_op jit(solution)/shard_map/ppermute | solution.py:15
  93.3 0.8 fusion.55
  94.4 10.9 %collective-permute-done.8 = bf16[8,4,8,768]{3,2,1,0:T(8,128)(2,1)} collective-permute-done((bf16[8,4,8,768]{3,2,1,0:T(8,128)(2,1)}, bf16[8,4,8,768]{3,2,1,0:T(8,128)(2,1)}, u32[]{:S(2)}, u32[]{:S(2)}) %collective-permute-start.8) | collective-permute-done | bytes 393248 | tf_op jit(solution)/shard_map/ppermute | solution.py:15
  105.3 1.1 pad_maximum_fusion.3
  106.4 0.6 fusion.49
  107.1 27.5 %while.31 = (s32[]{:T(128)}, bf16[1,512,1152]{1,2,0:T(8,128)(2,1)S(1)}, bf16[1,512,1152]{2,1,0:T(8,128)(2,1)S(1)}, bf16[1,512,384]{2,1,0:T(8,128)(2,1)S(1)}, s32...) while((s32[]{:T(128)}, ...), condition=%wide.region_10.11_spmd, body=%wide.region_6.10_spmd.sunk | while | flops 88160776 | bytes 9951540 | solution.py:155
  107.7 0.4 multiply_reduce_fusion.2
  109.4 0.4 fusion.100
  110.0 0.4 multiply_reduce_fusion.2
  111.7 0.4 fusion.100
  112.3 0.4 multiply_reduce_fusion.2
  114.6 0.4 multiply_reduce_fusion.2
  116.2 0.4 fusion.100
  116.8 0.4 multiply_reduce_fusion.2
  118.5 0.4 fusion.100
  119.1 0.4 multiply_reduce_fusion.2
  121.4 0.4 multiply_reduce_fusion.2
  123.1 0.4 fusion.100
  123.7 0.4 multiply_reduce_fusion.2
  126.0 0.4 multiply_reduce_fusion.2
  127.7 0.4 fusion.100
  128.3 0.4 multiply_reduce_fusion.2
  130.0 0.4 fusion.100
  130.6 0.4 multiply_reduce_fusion.2
  132.2 0.4 fusion.100
  132.9 0.4 multiply_reduce_fusion.2
  134.5 3.0 %fusion.50 = f32[768,1152]{1,0:T(8,128)} fusion(bf16[512,768]{1,0:T(8,128)(2,1)S(1)} %bitcast.108, bf16[1,512,1152]{1,2,0:T(8,128)(2,1)S(1)} %get-tuple-element.203), kind=kOutput, calls=%fused_computation.66 | convolution fusion | flops 905969664 | bytes 5505024 | tf_op jit(solution)/shard_map/dot_general | solution.py:164
  137.6 139.8 %all-reduce.2.cloned.1.call-done = f32[768,1152]{1,0:T(8,128)} async-done(((f32[768,1152]{1,0:T(8,128)}), f32[768,1152]{1,0:T(8,128)}) %all-reduce.2.cloned.1.call-update) | async-done | bytes 3538960 | tf_op jit(solution)/shard_map/psum | solution.py:167
  277.4 2.1 constant_dynamic-slice_fusion
  (139 shorter events, 33.6 us)
Async XLA Ops:
  7.2 2.1 copy-start
  7.2 2.5 copy-start.3
  7.2 43.5 %all-gather.2.cloned.1.call-start = ((), (), s32[]{:S(2)}) async-start(), calls=%async_computation | async-start | bytes 2211840 | tf_op jit(solution)/shard_map/all_gather | solution.py:78
  7.9 269.5 %all-reduce.2.cloned.1.call-start = ((), (), s32[]{:S(2)}) async-start(), calls=%async_computation.1 | async-start | bytes 7077888 | tf_op jit(solution)/shard_map/psum | solution.py:167
  10.3 5.0 %copy-start.2 = (bf16[96,768]{1,0:T(8,128)(2,1)S(1)}, bf16[96,768]{1,0:T(8,128)(2,1)}, u32[]{:S(2)}) copy-start(bf16[96,768]{1,0:T(8,128)(2,1)} %param.13) | copy-start | bytes 442372
  10.7 20.8 %collective-permute-start = (bf16[4,8,8,768]{3,2,1,0:T(8,128)(2,1)S(1)}, bf16[4,8,8,768]{3,2,1,0:T(8,128)(2,1)S(1)}, u32[]{:S(2)}, u32[]{:S(2)}) collective-permute-start(bf16[4,8,8,768]{3,2,1,0:T(8,128)(2,1)S(1)} %get-tuple-element.239), channel_id=1, source_target_pairs={{0,28},{4,0},{8,4},{12,8},{16,12},{20,16},{24,20},{28,24},{1,29},{... | collective-permute-start | bytes 1179656 | tf_op jit(solution)/shard_map/ppermute | solution.py:15
  15.3 6.4 %collective-permute-start.2 = (bf16[96,768]{1,0:T(8,128)(2,1)S(1)}, bf16[96,768]{1,0:T(8,128)(2,1)S(1)}, u32[]{:S(2)}, u32[]{:S(2)}) collective-permute-start(bf16[96,768]{1,0:T(8,128)(2,1)S(1)} %copy-done.2), channel_id=1, source_target_pairs={{0,1},{1,2},{2,3},{3,0},{4,5},{5,6},{6,7},{7,4},{8,9},{9,10},{10,1... | collective-permute-start | bytes 442376 | tf_op jit(solution)/shard_map/ppermute | solution.py:100
  21.7 9.8 %collective-permute-start.3 = (bf16[96,768]{1,0:T(8,128)(2,1)S(1)}, bf16[96,768]{1,0:T(8,128)(2,1)S(1)}, u32[]{:S(2)}, u32[]{:S(2)}) collective-permute-start(bf16[96,768]{1,0:T(8,128)(2,1)S(1)} %collective-permute-done.2), channel_id=1, source_target_pairs={{0,1},{1,2},{2,3},{3,0},{4,5},{5,6},{6,7},{7,4},{8,9},{9,10},{10,1... | collective-permute-start | bytes 442376 | tf_op jit(solution)/shard_map/ppermute | solution.py:100
  31.5 6.0 %collective-permute-start.4 = (bf16[96,768]{1,0:T(8,128)(2,1)S(1)}, bf16[96,768]{1,0:T(8,128)(2,1)S(1)}, u32[]{:S(2)}, u32[]{:S(2)}) collective-permute-start(bf16[96,768]{1,0:T(8,128)(2,1)S(1)} %collective-permute-done.3), channel_id=1, source_target_pairs={{0,1},{1,2},{2,3},{3,0},{4,5},{5,6},{6,7},{7,4},{8,9},{9,10},{10,1... | collective-permute-start | bytes 442376 | tf_op jit(solution)/shard_map/ppermute | solution.py:100
  31.6 16.4 %collective-permute-start.1 = (bf16[8,4,8,768]{3,2,1,0:T(8,128)(2,1)S(1)}, bf16[8,4,8,768]{3,2,1,0:T(8,128)(2,1)S(1)}, u32[]{:S(2)}, u32[]{:S(2)}) collective-permute-start(bf16[8,4,8,768]{3,2,1,0:T(8,128)(2,1)S(1)} %get-tuple-element.237), channel_id=1, source_target_pairs={{0,3},{1,0},{2,1},{3,2},{4,7},{5,4},{6,5},{7,6},{8,11},{9,8},{10,9... | collective-permute-start | bytes 1179656 | tf_op jit(solution)/shard_map/ppermute | solution.py:15
  65.2 10.0 %collective-permute-start.5 = (bf16[4,8,8,768]{3,2,1,0:T(8,128)(2,1)S(1)}, bf16[4,8,8,768]{3,2,1,0:T(8,128)(2,1)S(1)}, u32[]{:S(2)}, u32[]{:S(2)}) collective-permute-start(bf16[4,8,8,768]{3,2,1,0:T(8,128)(2,1)S(1)} %bitcast.112), channel_id=1, source_target_pairs={{0,4},{4,8},{8,12},{12,16},{16,20},{20,24},{24,28},{28,0},{1,5},{5... | collective-permute-start | bytes 1179656 | tf_op jit(solution)/shard_map/ppermute | solution.py:15
  75.3 9.3 %collective-permute-start.6 = (bf16[8,4,8,768]{3,2,1,0:T(8,128)(2,1)S(1)}, bf16[8,4,8,768]{3,2,1,0:T(8,128)(2,1)S(1)}, u32[]{:S(2)}, u32[]{:S(2)}) collective-permute-start(bf16[8,4,8,768]{3,2,1,0:T(8,128)(2,1)S(1)} %fusion.57), channel_id=1, source_target_pairs={{0,1},{1,2},{2,3},{3,0},{4,5},{5,6},{6,7},{7,4},{8,9},{9,10},{10,1... | collective-permute-start | bytes 1179656 | tf_op jit(solution)/shard_map/ppermute | solution.py:15
  84.6 1.1 copy-start.1
  88.0 5.4 %collective-permute-start.7 = (bf16[4,8,8,768]{3,2,1,0:T(8,128)(2,1)S(1)}, bf16[4,8,8,768]{3,2,1,0:T(8,128)(2,1)S(1)}, u32[]{:S(2)}, u32[]{:S(2)}) collective-permute-start(bf16[4,8,8,768]{3,2,1,0:T(8,128)(2,1)S(1)} %get-tuple-element.229), channel_id=1, source_target_pairs={{0,28},{4,0},{8,4},{12,8},{16,12},{20,16},{24,20},{28,24},{1,29},{... | collective-permute-start | bytes 1179656 | tf_op jit(solution)/shard_map/ppermute | solution.py:15
  94.1 11.2 %collective-permute-start.8 = (bf16[8,4,8,768]{3,2,1,0:T(8,128)(2,1)}, bf16[8,4,8,768]{3,2,1,0:T(8,128)(2,1)}, u32[]{:S(2)}, u32[]{:S(2)}) collective-permute-start(bf16[8,4,8,768]{3,2,1,0:T(8,128)(2,1)} %get-tuple-element.227), channel_id=1, source_target_pairs={{0,3},{1,0},{2,1},{3,2},{4,7},{5,4},{6,5},{7,6},{8,11},{9,8},{10,9... | collective-permute-start | bytes 1179656 | tf_op jit(solution)/shard_map/ppermute | solution.py:15
Sparse Core Ops, SparseCore 0:
  9.8 40.8 all-gather.1
  137.7 139.6 all-reduce.1
